TPU v7x, 256 devices: a whole 4x4x8 slice. The times are simulated.
256 devices in a mesh: grp: 32 (over x, y, core), blk: 8 (over z).
Axes of the slice: x: 4, y: 4, z: 8, core: 2. Of those that a mesh axis runs over, the one named last changes fastest.
Arguments:
- tiles_near: bfloat16 [16384, 256, 256], P(('grp', 'blk')), may hold values from -0.078125 to 0.078125
- near_cols: int32 [256, 64], P(('grp', 'blk')), may hold values from 0 to 3
- tiles_far: bfloat16 [6144, 256, 256], P(('grp', 'blk')), may hold values from -0.078125 to 0.078125
- far_groups: int32 [256, 24], P(('grp', 'blk')), may hold values from 0 to 31, as said below
- need_blocks: int32 [256, 32], P(('grp', 'blk')), may hold values from -1 to 3, as said below
- start_vectors: bfloat16 [262144, 128], P(('grp', 'blk')), may hold values from -6 to 6
Outputs:
- vectors: float32 [262144, 128], P(('grp', 'blk'))
Inputs may be any that keep to these rules, and one draw needn't show every extreme that they name: need_blocks[d, h] is -1 for d's own group and for groups d reads nothing from, else a row block index below 4 of the device of group h at d's position along blk; every device reads from at least one other group. far_groups[d, t] is a group h with need_blocks[d, h] >= 0.
All inputs are finite; a program needn't handle non-finite values.
Results may differ from a plain program's by a relative error of at most 0.0029.
Values may be sent and summed in bfloat16 or wider, within the bound.
A program may use at most 128 MiB of HBM per device.

v0:
```python
import jax
import jax.numpy as jnp
from jax import lax
from jax.sharding import PartitionSpec as P

ITERS = 2


def per_device(tiles_near, near_cols, tiles_far, far_groups, need_blocks, start_vectors):
    tile_size = tiles_near.shape[1]
    vec_width = start_vectors.shape[1]
    blocks = start_vectors.shape[0] // tile_size
    group_size = lax.axis_size("blk")
    group_count = lax.axis_size("grp")
    per_source = tiles_near.shape[0] // (blocks * group_size)
    far_each = tiles_far.shape[0] // blocks
    near_tiles = tiles_near.reshape(blocks, group_size, per_source, tile_size, tile_size)
    near_index = near_cols.reshape(blocks, group_size, per_source)
    far_tiles = tiles_far.reshape(blocks, far_each, tile_size, tile_size)
    far_index = far_groups.reshape(blocks, far_each)
    wanted = need_blocks.reshape(group_count)
    total_rows = blocks * tile_size * group_size * group_count
    current = start_vectors
    vectors = start_vectors.astype(jnp.float32)
    for iteration in range(ITERS):
        local_rows = current.reshape(blocks, tile_size, vec_width)
        group_table = lax.all_gather(local_rows, "blk", axis=0, tiled=True)
        source_ids = jnp.arange(group_size, dtype=jnp.int32)[None, :, None]
        chosen = group_table[source_ids * blocks + near_index]
        near_part = jnp.einsum(
            "rmnij,rmnjk->rik", near_tiles, chosen, preferred_element_type=jnp.float32
        )
        everything = lax.all_gather(local_rows, "grp", axis=0, tiled=True)
        far_rows = everything[far_index * blocks + wanted[far_index]]
        far_part = jnp.einsum(
            "rnij,rnjk->rik", far_tiles, far_rows, preferred_element_type=jnp.float32
        )
        product = near_part + far_part
        flat_rows = product.reshape(blocks * tile_size, vec_width)
        local_gram = jnp.dot(
            flat_rows.T,
            flat_rows,
            precision=lax.Precision.HIGHEST,
            preferred_element_type=jnp.float32,
        )
        gram = lax.psum(local_gram, ("grp", "blk")) / total_rows
        factor = jnp.linalg.cholesky(gram)
        identity_matrix = jnp.eye(vec_width, dtype=jnp.float32)
        inverse = lax.linalg.triangular_solve(factor, identity_matrix, left_side=True, lower=True).T
        vectors = jnp.dot(
            flat_rows, inverse, precision=lax.Precision.HIGHEST, preferred_element_type=jnp.float32
        )
        current = vectors.astype(jnp.bfloat16)
    return vectors


def solution(mesh):
    in_specs = (
        P(("grp", "blk"), None, None),
        P(("grp", "blk"), None),
        P(("grp", "blk"), None, None),
        P(("grp", "blk"), None),
        P(("grp", "blk"), None),
        P(("grp", "blk"), None),
    )
    out_specs = P(("grp", "blk"), None)
    return jax.shard_map(
        per_device, mesh=mesh, in_specs=in_specs, out_specs=out_specs, check_vma=False
    )
```

profile of v0, /device:TPU:1, one launch (start us, length us, event | category | flops | bytes accessed | tf_op | source)
XLA Modules:
  0.0 777.3 jit_solution(7489281376360508679)
XLA Ops:
  6.5 0.0 copy-start
  6.5 0.7 all-gather.5.cloned.1.call-update
  7.3 0.0 all-gather.7.cloned.1.call-start
  7.3 0.7 all-gather.7.cloned.1.call-update
  8.0 0.0 all-reduce.3.cloned.1.call-start
  8.1 0.5 broadcast.166
  8.6 1.3 reduce.10
  9.9 0.1 reshape.119
  10.0 0.1 reshape.137
  10.1 1.4 gather_fusion.1
  11.4 0.1 gather.20
  11.5 0.1 reshape.145
  11.6 1.3 reduce.11
  12.9 0.1 reshape.117
  13.1 0.1 compare_select_fusion
  13.1 0.1 reshape.129
  13.3 37.1 %all-gather.5.cloned.1.call-done = bf16[32,256,128]{2,1,0:T(8,128)(2,1)} async-done(((bf16[4,256,128]{2,1,0:T(8,128)(2,1)}), bf16[32,256,128]{2,1,0:T(8,128)(2,1)}) %all-gather.5.cloned.1.call-update) | async-done | bytes 2097168 | tf_op jit(solution)/shard_map/all_gather | solution.py:27
  50.4 4.6 gather_fusion
  55.0 58.5 %all-gather.7.cloned.1.call-done = bf16[128,256,128]{2,1,0:T(8,128)(2,1)} async-done(((bf16[4,256,128]{2,1,0:T(8,128)(2,1)}), bf16[128,256,128]{2,1,0:T(8,128)(2,1)}) %all-gather.7.cloned.1.call-update) | async-done | bytes 8388624 | tf_op jit(solution)/shard_map/all_gather | solution.py:33
  113.6 5.4 gather_fusion.2
  118.9 2.7 convolution_bitcast_fusion.1
  121.7 0.0 copy-done.4
  121.7 5.2 fusion.31
  126.9 0.0 copy-start.1
  126.9 0.8 copy-done.1
  127.7 1.2 convolution_bitcast_fusion.3
  128.9 0.0 all-reduce.3.cloned.1.call-update
  128.9 0.0 all-gather.9.cloned.1.call-start
  129.0 2.0 copy.32
  131.0 235.3 %all-reduce.3.cloned.1.call-done = f32[128,128]{0,1:T(8,128)} async-done(((f32[128,128]{0,1:T(8,128)}), f32[128,128]{0,1:T(8,128)}) %all-reduce.3.cloned.1.call-update) | async-done | bytes 65552 | tf_op jit(solution)/shard_map/psum | solution.py:46
  366.3 0.8 broadcast_multiply_fusion.1
  367.2 0.1 copy.35
  367.3 0.9 fusion.45
  368.1 11.7 %cholesky.44 = f32[128,128]{1,0:T(8,128)S(1)} custom-call(f32[128,128]{1,0:T(8,128)S(1)} %fusion.45), custom_call_target="Cholesky" | custom-call | tf_op jit(solution)/shard_map/jit(cholesky)/cholesky | solution.py:47
  379.9 0.6 compare_reduce_fusion.1
  380.5 0.7 fusion.40
  381.2 9.8 %custom-call.6 = f32[1,128,128]{1,2,0:T(8,128)S(1)} custom-call(f32[1,128,128]{2,1,0:T(8,128)S(1)} %fusion.40), custom_call_target="InvertDiagBlocksLowerTriangular" | custom-call | tf_op jit(solution)/shard_map/triangular_solve/custom-call.0 | solution.py:49
  391.0 0.3 fusion.38
  391.3 2.3 convolution_convert_fusion
  393.6 0.0 all-gather.9.cloned.1.call-update
  393.6 0.0 all-gather.11.cloned.1.call-start
  393.7 0.5 all-gather.11.cloned.1.call-update
  394.2 0.2 all-reduce.5.cloned.1.call-start
  394.5 32.8 %all-gather.9.cloned.1.call-done = bf16[32,256,128]{2,1,0:T(8,128)(2,1)} async-done(((bf16[4,256,128]{2,1,0:T(8,128)(2,1)}), bf16[32,256,128]{2,1,0:T(8,128)(2,1)}) %all-gather.9.cloned.1.call-update) | async-done | bytes 2097168 | tf_op jit(solution)/shard_map/all_gather | solution.py:27
  427.3 4.6 gather_fusion.3
  432.0 58.4 %all-gather.11.cloned.1.call-done = bf16[128,256,128]{2,1,0:T(8,128)(2,1)} async-done(((bf16[4,256,128]{2,1,0:T(8,128)(2,1)}), bf16[128,256,128]{2,1,0:T(8,128)(2,1)}) %all-gather.11.cloned.1.call-update) | async-done | bytes 8388624 | tf_op jit(solution)/shard_map/all_gather | solution.py:33
  490.3 5.4 gather_fusion.4
  495.7 2.7 convolution_bitcast_fusion
  498.4 5.2 fusion.21
  503.7 0.0 copy-start.2
  503.7 0.8 copy-done.2
  504.5 1.2 convolution_bitcast_fusion.2
  505.7 0.0 all-reduce.5.cloned.1.call-update
  505.7 2.0 copy.39
  507.7 235.3 %all-reduce.5.cloned.1.call-done = f32[128,128]{0,1:T(8,128)} async-done(((f32[128,128]{0,1:T(8,128)}), f32[128,128]{0,1:T(8,128)}) %all-reduce.5.cloned.1.call-update) | async-done | bytes 65552 | tf_op jit(solution)/shard_map/psum | solution.py:46
  743.1 0.8 broadcast_multiply_fusion
  743.9 0.1 copy.42
  744.0 0.9 fusion.43
  744.9 11.7 %cholesky.55 = f32[128,128]{1,0:T(8,128)S(1)} custom-call(f32[128,128]{1,0:T(8,128)S(1)} %fusion.43), custom_call_target="Cholesky" | custom-call | tf_op jit(solution)/shard_map/jit(cholesky)/cholesky | solution.py:47
  756.6 0.6 compare_reduce_fusion
  757.2 0.7 fusion.41
  757.9 9.8 %custom-call.7 = f32[1,128,128]{1,2,0:T(8,128)S(1)} custom-call(f32[1,128,128]{2,1,0:T(8,128)S(1)} %fusion.41), custom_call_target="InvertDiagBlocksLowerTriangular" | custom-call | tf_op jit(solution)/shard_map/triangular_solve/custom-call.0 | solution.py:49
  767.7 0.3 fusion.36
  768.0 2.4 fusion.46
  (13 shorter events, 0.1 us)
Async XLA Ops:
  6.5 112.4 %copy-start = (bf16[24,256,256]{2,1,0:T(8,128)(2,1)S(1)}, bf16[24,256,256]{2,1,0:T(8,128)(2,1)}, u32[]{:S(2)}) copy-start(bf16[24,256,256]{2,1,0:T(8,128)(2,1)} %param.11) | copy-start | bytes 9437188
  6.5 43.8 %all-gather.5.cloned.1.call-start = ((), (), s32[]{:S(2)}) async-start(), calls=%async_computation | async-start | bytes 2359296 | tf_op jit(solution)/shard_map/all_gather | solution.py:27
  7.3 106.3 %all-gather.7.cloned.1.call-start = ((), (), s32[]{:S(2)}) async-start(), calls=%async_computation.1 | async-start | bytes 8650752 | tf_op jit(solution)/shard_map/all_gather | solution.py:33
  8.0 358.3 %all-reduce.3.cloned.1.call-start = ((), (), s32[]{:S(2)}) async-start(), calls=%async_computation.2 | async-start | bytes 131072 | tf_op jit(solution)/shard_map/psum | solution.py:46
  118.9 2.7 copy-start.4
  126.9 0.8 copy-start.1
  128.9 298.4 %all-gather.9.cloned.1.call-start = ((), (), s32[]{:S(2)}) async-start(), calls=%async_computation.3 | async-start | bytes 2359296 | tf_op jit(solution)/shard_map/all_gather | solution.py:27
  393.6 96.7 %all-gather.11.cloned.1.call-start = ((), (), s32[]{:S(2)}) async-start(), calls=%async_computation.4 | async-start | bytes 8650752 | tf_op jit(solution)/shard_map/all_gather | solution.py:33
  394.2 348.8 %all-reduce.5.cloned.1.call-start = ((), (), s32[]{:S(2)}) async-start(), calls=%async_computation.5 | async-start | bytes 131072 | tf_op jit(solution)/shard_map/psum | solution.py:46
  495.7 2.7 copy-start.3
  503.7 0.8 copy-start.2
Sparse Core Ops, SparseCore 0:
  9.1 41.1 all-gather.4
  52.9 60.5 all-gather.6
  129.1 237.2 all-reduce.2
  393.8 33.4 all-gather.8
  429.7 60.5 all-gather.10
  505.8 237.1 all-reduce.4
where the time goes:
time: 778 us; the launch traced here: 777 us
  waiting for transfers between devices  659 us (85%)
  other arithmetic  51.9 us (7%)
  local copies, waits for them, and re-layouts  28.3 us (4%)
  matrix products  23.6 us (3%)
  between operations  13.7 us (2%)
    psum x2, waiting for transfers between devices, per_device(): gram = lax.psum(local_gram, ('grp', 'blk')) / total_rows  471 us
    all_gather x2, waiting for transfers between devices, per_device(): everything = lax.all_gather(local_rows, 'grp', axis=0, tiled=True)  117 us
    all_gather x2, waiting for transfers between devices, per_device(): group_table = lax.all_gather(local_rows, 'blk', axis=0, tiled=True)  70 us
    another operation x6, other arithmetic, per_device(): factor = jnp.linalg.cholesky(gram)  24.8 us
    another operation x4, other arithmetic, per_device(): lax.linalg.triangular_solve(factor, identity_matrix, left_side=True, lowe...  20.9 us
  transfers between devices with their start and end apart: 6, of which 6 were waited for; matrix products, arithmetic and copies ran while one was open for 2% of the time, Pallas kernels for 0%

commit v1 on v0

--- a/solution.py
+++ b/solution.py
@@ -43,7 +43,7 @@
             precision=lax.Precision.HIGHEST,
             preferred_element_type=jnp.float32,
         )
-        gram = lax.psum(local_gram, ("grp", "blk")) / total_rows
+        gram = lax.psum(lax.psum(local_gram, "blk"), "grp") / total_rows
         factor = jnp.linalg.cholesky(gram)
         identity_matrix = jnp.eye(vec_width, dtype=jnp.float32)
         inverse = lax.linalg.triangular_solve(factor, identity_matrix, left_side=True, lower=True).T

time: 778 us -> 663 us (0.85)
  waiting for transfers between devices: 659 us -> 545 us
    psum x2 -> x4, waiting for transfers between devices: 471 us -> 353 us  [per_device(): gram = lax.psum(lax.psum(local_gram, 'blk'), 'grp') / total_rows]
  transfers between devices with their start and end apart: 6 -> 8, of which waited for: 6 -> 8; matrix products, arithmetic and copies ran while one was open for 2% -> 3% of each run, Pallas kernels for 0% -> 0%
where the time goes in v1:
time: 663 us
  waiting for transfers between devices  545 us (82%)
  other arithmetic  51.9 us (8%)
  local copies, waits for them, and re-layouts  28.3 us (4%)
  matrix products  23.6 us (4%)
  between operations  13.7 us (2%)
    psum x4, waiting for transfers between devices, per_device(): gram = lax.psum(lax.psum(local_gram, 'blk'), 'grp') / total_rows  353 us
    all_gather x2, waiting for transfers between devices, per_device(): everything = lax.all_gather(local_rows, 'grp', axis=0, tiled=True)  117 us
    all_gather x2, waiting for transfers between devices, per_device(): group_table = lax.all_gather(local_rows, 'blk', axis=0, tiled=True)  72.5 us
    another operation x6, other arithmetic, per_device(): factor = jnp.linalg.cholesky(gram)  24.8 us
    another operation x4, other arithmetic, per_device(): lax.linalg.triangular_solve(factor, identity_matrix, left_side=True, lowe...  20.9 us
  transfers between devices with their start and end apart: 8, of which 8 were waited for; matrix products, arithmetic and copies ran while one was open for 3% of the time, Pallas kernels for 0%

profile of v1, /device:TPU:1, one launch (start us, length us, event | category | flops | bytes accessed | tf_op | source)
XLA Modules:
  0.0 662.7 jit_solution(17956715218961829974)
XLA Ops:
  6.5 0.7 all-gather.5.cloned.1.call-update
  7.3 0.0 all-gather.7.cloned.1.call-start
  7.3 0.7 all-gather.7.cloned.1.call-update
  8.0 0.0 all-reduce.5.cloned.1.call-start
  8.1 0.5 broadcast.166
  8.6 1.3 reduce.10
  9.9 0.1 reshape.119
  10.0 0.1 reshape.137
  10.1 1.4 gather_fusion.1
  11.4 0.1 gather.20
  11.5 0.1 reshape.145
  11.6 1.3 reduce.11
  12.9 0.1 reshape.117
  13.1 0.1 compare_select_fusion
  13.1 0.1 reshape.129
  13.3 37.1 %all-gather.5.cloned.1.call-done = bf16[32,256,128]{2,1,0:T(8,128)(2,1)} async-done(((bf16[4,256,128]{2,1,0:T(8,128)(2,1)}), bf16[32,256,128]{2,1,0:T(8,128)(2,1)}) %all-gather.5.cloned.1.call-update) | async-done | bytes 2097168 | tf_op jit(solution)/shard_map/all_gather | solution.py:27
  50.4 4.6 gather_fusion
  55.0 58.5 %all-gather.7.cloned.1.call-done = bf16[128,256,128]{2,1,0:T(8,128)(2,1)} async-done(((bf16[4,256,128]{2,1,0:T(8,128)(2,1)}), bf16[128,256,128]{2,1,0:T(8,128)(2,1)}) %all-gather.7.cloned.1.call-update) | async-done | bytes 8388624 | tf_op jit(solution)/shard_map/all_gather | solution.py:33
  113.6 5.4 gather_fusion.2
  118.9 2.7 convolution_bitcast_fusion.1
  121.7 5.2 fusion.31
  126.9 0.8 copy-done.1
  127.7 1.2 convolution_bitcast_fusion.3
  128.9 0.0 all-reduce.7.cloned.1.call-start
  129.0 65.8 %all-reduce.5.cloned.1.call-done = f32[128,128]{0,1:T(8,128)} async-done(((f32[128,128]{0,1:T(8,128)}), f32[128,128]{0,1:T(8,128)}) %all-reduce.5.cloned.1.call-update) | async-done | bytes 65552 | tf_op jit(solution)/shard_map/psum | solution.py:46
  194.8 0.0 all-reduce.7.cloned.1.call-update
  194.8 0.0 all-gather.9.cloned.1.call-start
  194.9 2.0 copy.32
  196.9 110.8 %all-reduce.7.cloned.1.call-done = f32[128,128]{0,1:T(8,128)} async-done(((f32[128,128]{0,1:T(8,128)}), f32[128,128]{0,1:T(8,128)}) %all-reduce.7.cloned.1.call-update) | async-done | bytes 65552 | tf_op jit(solution)/shard_map/psum | solution.py:46
  307.7 0.8 broadcast_multiply_fusion.1
  308.5 0.1 copy.35
  308.6 0.9 fusion.45
  309.5 11.7 %cholesky.44 = f32[128,128]{1,0:T(8,128)S(1)} custom-call(f32[128,128]{1,0:T(8,128)S(1)} %fusion.45), custom_call_target="Cholesky" | custom-call | tf_op jit(solution)/shard_map/jit(cholesky)/cholesky | solution.py:47
  321.2 0.6 compare_reduce_fusion.1
  321.9 0.7 fusion.40
  322.5 9.8 %custom-call.6 = f32[1,128,128]{1,2,0:T(8,128)S(1)} custom-call(f32[1,128,128]{2,1,0:T(8,128)S(1)} %fusion.40), custom_call_target="InvertDiagBlocksLowerTriangular" | custom-call | tf_op jit(solution)/shard_map/triangular_solve/custom-call.0 | solution.py:49
  332.3 0.3 fusion.38
  332.6 2.3 convolution_convert_fusion
  335.0 0.0 all-gather.9.cloned.1.call-update
  335.0 0.0 all-gather.11.cloned.1.call-start
  335.0 0.5 all-gather.11.cloned.1.call-update
  335.6 0.2 all-reduce.9.cloned.1.call-start
  335.8 35.4 %all-gather.9.cloned.1.call-done = bf16[32,256,128]{2,1,0:T(8,128)(2,1)} async-done(((bf16[4,256,128]{2,1,0:T(8,128)(2,1)}), bf16[32,256,128]{2,1,0:T(8,128)(2,1)}) %all-gather.9.cloned.1.call-update) | async-done | bytes 2097168 | tf_op jit(solution)/shard_map/all_gather | solution.py:27
  371.2 4.6 gather_fusion.3
  375.9 58.4 %all-gather.11.cloned.1.call-done = bf16[128,256,128]{2,1,0:T(8,128)(2,1)} async-done(((bf16[4,256,128]{2,1,0:T(8,128)(2,1)}), bf16[128,256,128]{2,1,0:T(8,128)(2,1)}) %all-gather.11.cloned.1.call-update) | async-done | bytes 8388624 | tf_op jit(solution)/shard_map/all_gather | solution.py:33
  434.2 5.4 gather_fusion.4
  439.6 2.7 convolution_bitcast_fusion
  442.4 5.2 fusion.21
  447.6 0.8 copy-done.2
  448.4 1.2 convolution_bitcast_fusion.2
  449.6 0.0 all-reduce.9.cloned.1.call-update
  449.6 0.0 all-reduce.11.cloned.1.call-start
  449.7 65.8 %all-reduce.9.cloned.1.call-done = f32[128,128]{0,1:T(8,128)} async-done(((f32[128,128]{0,1:T(8,128)}), f32[128,128]{0,1:T(8,128)}) %all-reduce.9.cloned.1.call-update) | async-done | bytes 65552 | tf_op jit(solution)/shard_map/psum | solution.py:46
  515.5 2.0 copy.39
  517.5 110.9 %all-reduce.11.cloned.1.call-done = f32[128,128]{0,1:T(8,128)} async-done(((f32[128,128]{0,1:T(8,128)}), f32[128,128]{0,1:T(8,128)}) %all-reduce.11.cloned.1.call-update) | async-done | bytes 65552 | tf_op jit(solution)/shard_map/psum | solution.py:46
  628.5 0.8 broadcast_multiply_fusion
  629.3 0.1 copy.42
  629.4 0.9 fusion.43
  630.3 11.7 %cholesky.55 = f32[128,128]{1,0:T(8,128)S(1)} custom-call(f32[128,128]{1,0:T(8,128)S(1)} %fusion.43), custom_call_target="Cholesky" | custom-call | tf_op jit(solution)/shard_map/jit(cholesky)/cholesky | solution.py:47
  642.0 0.6 compare_reduce_fusion
  642.7 0.7 fusion.41
  643.3 9.8 %custom-call.7 = f32[1,128,128]{1,2,0:T(8,128)S(1)} custom-call(f32[1,128,128]{2,1,0:T(8,128)S(1)} %fusion.41), custom_call_target="InvertDiagBlocksLowerTriangular" | custom-call | tf_op jit(solution)/shard_map/triangular_solve/custom-call.0 | solution.py:49
  653.1 0.3 fusion.36
  653.4 2.4 fusion.46
  (19 shorter events, 0.2 us)
Async XLA Ops:
  6.5 112.4 %copy-start = (bf16[24,256,256]{2,1,0:T(8,128)(2,1)S(1)}, bf16[24,256,256]{2,1,0:T(8,128)(2,1)}, u32[]{:S(2)}) copy-start(bf16[24,256,256]{2,1,0:T(8,128)(2,1)} %param.11) | copy-start | bytes 9437188
  6.5 43.8 %all-gather.5.cloned.1.call-start = ((), (), s32[]{:S(2)}) async-start(), calls=%async_computation | async-start | bytes 2359296 | tf_op jit(solution)/shard_map/all_gather | solution.py:27
  7.3 106.3 %all-gather.7.cloned.1.call-start = ((), (), s32[]{:S(2)}) async-start(), calls=%async_computation.1 | async-start | bytes 8650752 | tf_op jit(solution)/shard_map/all_gather | solution.py:33
  8.0 186.8 %all-reduce.5.cloned.1.call-start = ((), (), s32[]{:S(2)}) async-start(), calls=%async_computation.2 | async-start | bytes 131072 | tf_op jit(solution)/shard_map/psum | solution.py:46
  118.9 2.7 copy-start.4
  126.9 0.8 copy-start.1
  128.9 178.7 %all-reduce.7.cloned.1.call-start = ((), (), s32[]{:S(2)}) async-start(), calls=%async_computation.3 | async-start | bytes 131072 | tf_op jit(solution)/shard_map/psum | solution.py:46
  194.8 176.4 %all-gather.9.cloned.1.call-start = ((), (), s32[]{:S(2)}) async-start(), calls=%async_computation.4 | async-start | bytes 2359296 | tf_op jit(solution)/shard_map/all_gather | solution.py:27
  335.0 99.3 %all-gather.11.cloned.1.call-start = ((), (), s32[]{:S(2)}) async-start(), calls=%async_computation.5 | async-start | bytes 8650752 | tf_op jit(solution)/shard_map/all_gather | solution.py:33
  335.6 179.9 %all-reduce.9.cloned.1.call-start = ((), (), s32[]{:S(2)}) async-start(), calls=%async_computation.6 | async-start | bytes 131072 | tf_op jit(solution)/shard_map/psum | solution.py:46
  439.6 2.7 copy-start.3
  447.6 0.8 copy-start.2
  449.6 178.9 %all-reduce.11.cloned.1.call-start = ((), (), s32[]{:S(2)}) async-start(), calls=%async_computation.7 | async-start | bytes 131072 | tf_op jit(solution)/shard_map/psum | solution.py:46
Sparse Core Ops, SparseCore 0:
  9.1 41.1 all-gather.4
  52.9 60.5 all-gather.6
  129.1 65.6 all-reduce.4
  198.3 109.3 all-reduce.6
  335.1 36.0 all-gather.8
  373.6 60.5 all-gather.10
  449.7 65.6 all-reduce.8
  519.1 109.3 all-reduce.10
